TPU v7x, 256 devices: a whole 4x4x8 slice. The times are simulated.
256 devices in a mesh: row: 32 (over z, y), col: 8 (over x, core).
Axes of the slice: x: 4, y: 4, z: 8, core: 2. Of those that a mesh axis runs over, the one named last changes fastest.
Arguments:
- covariance: float32 [16384, 16384], P('row', 'col'), as said below
- courant: float32 [2, 16384], replicated, may hold values from 0.05 to 0.45
- upwind: int32 [16384], replicated, may hold values from 0 to 3
- observed: int32 [2, 256], replicated, may hold values from 0 to 16383
- noise: float32 [2, 256], replicated, may hold values from 0.5 to 2
Outputs:
- posterior: float32 [16384, 16384], P('row', 'col')
Inputs may be any that keep to these rules, and one draw needn't show every extreme that they name: The covariance is symmetric and positive definite.
All inputs are finite; a program needn't handle non-finite values.
Results may differ from a plain program's by a relative error of at most 0.0003.
Values sent between devices are 32-bit elements; how exact they have to be, the bound alone decides.
No kernel may reach another device: no remote copies, remote signals or barrier semaphores. Data moves between devices by JAX's collectives and lax.ppermute only.
A program may use at most 64 MiB of HBM per device.

v0:
```python
import jax
import jax.numpy as jnp
from jax import lax
from jax.sharding import PartitionSpec as P

G = 128
BATCHES = 2


def extended(block, sides, width):
    for axis, dim in sides:
        count = lax.axis_size(axis)
        forward = [(i, i + 1) for i in range(count - 1)]
        backward = [(target, source) for source, target in forward]
        low = lax.ppermute(
            lax.slice_in_dim(block, block.shape[dim] - width, None, axis=dim), axis, forward
        )
        high = lax.ppermute(lax.slice_in_dim(block, 0, width, axis=dim), axis, backward)
        block = jnp.concatenate([low, block, high], axis=dim)
    return block


def left_apply(padded, cour_a, cour_b, up_dir):
    lines = padded.shape[0] - 2
    center = padded[1:-1]
    prev_line = padded[:-2]
    next_line = padded[2:]
    prev_cell = jnp.pad(center, ((0, 0), (1, 0), (0, 0)))[:, :-1]
    next_cell = jnp.pad(center, ((0, 0), (0, 1), (0, 0)))[:, 1:]
    coef_a = cour_a.reshape(lines, G, 1)
    coef_b = cour_b.reshape(lines, G, 1)
    dirs = up_dir.reshape(lines, G, 1)
    up_line = jnp.where(dirs % 2 == 1, next_line, prev_line)
    up_cell = jnp.where(dirs // 2 == 1, next_cell, prev_cell)
    return (1.0 - coef_a - coef_b) * center + coef_a * up_line + coef_b * up_cell


def right_apply(padded, cour_a, cour_b, up_dir):
    lines = padded.shape[1] - 2
    center = padded[:, 1:-1]
    prev_line = padded[:, :-2]
    next_line = padded[:, 2:]
    prev_cell = jnp.pad(center, ((0, 0), (0, 0), (1, 0)))[:, :, :-1]
    next_cell = jnp.pad(center, ((0, 0), (0, 0), (0, 1)))[:, :, 1:]
    coef_a = cour_a.reshape(1, lines, G)
    coef_b = cour_b.reshape(1, lines, G)
    dirs = up_dir.reshape(1, lines, G)
    up_line = jnp.where(dirs % 2 == 1, next_line, prev_line)
    up_cell = jnp.where(dirs // 2 == 1, next_cell, prev_cell)
    return (1.0 - coef_a - coef_b) * center + coef_a * up_line + coef_b * up_cell


def transport(block, row_cour, row_dirs, col_cour, col_dirs):
    row_count, col_count = block.shape
    padded = extended(block, (("row", 0),), G)
    padded = padded.reshape(row_count // G + 2, G, col_count)
    block = left_apply(padded, row_cour[0], row_cour[1], row_dirs).reshape(row_count, col_count)
    padded = extended(block, (("col", 1),), G)
    padded = padded.reshape(row_count, col_count // G + 2, G)
    return right_apply(padded, col_cour[0], col_cour[1], col_dirs).reshape(row_count, col_count)


def shards(covariance, courant, upwind, observed, noise):
    row_count, col_count = covariance.shape
    row_start = lax.axis_index("row") * row_count
    col_start = lax.axis_index("col") * col_count
    row_cour = lax.dynamic_slice_in_dim(courant, row_start, row_count, 1)
    col_cour = lax.dynamic_slice_in_dim(courant, col_start, col_count, 1)
    row_dirs = lax.dynamic_slice_in_dim(upwind, row_start, row_count, 0)
    col_dirs = lax.dynamic_slice_in_dim(upwind, col_start, col_count, 0)
    block = covariance
    for cycle in range(BATCHES):
        block = transport(block, row_cour, row_dirs, col_cour, col_dirs)
        obs = observed[cycle]
        local_rows = obs - row_start
        owns_row = (local_rows >= 0) & (local_rows < row_count)
        row_pick = jnp.clip(local_rows, 0, row_count - 1)
        local_cols = obs - col_start
        owns_col = (local_cols >= 0) & (local_cols < col_count)
        col_pick = jnp.clip(local_cols, 0, col_count - 1)
        row_part = jnp.where(owns_row[:, None], jnp.take(block, row_pick, axis=0), 0.0)
        col_part = jnp.where(owns_col[None, :], jnp.take(block, col_pick, axis=1), 0.0)
        row_panel = lax.psum(row_part, "row")
        block_part = jnp.where(owns_col[None, :], jnp.take(row_panel, col_pick, axis=1), 0.0)
        col_panel, innov = lax.psum((col_part, block_part), "col")
        innov = innov + jnp.diag(noise[cycle])
        factor = jnp.linalg.cholesky(innov)
        gain = jax.scipy.linalg.cho_solve((factor, True), col_panel.T).T
        block = block - jnp.dot(
            gain, row_panel, precision=lax.Precision.HIGHEST, preferred_element_type=jnp.float32
        )
    return block


def solution(mesh):
    in_specs = (P("row", "col"), P(), P(), P(), P())
    out_specs = P("row", "col")
    return jax.shard_map(shards, mesh=mesh, in_specs=in_specs, out_specs=out_specs, check_vma=False)
```

profile of v0, /device:TPU:8, one launch (start us, length us, event | category | flops | bytes accessed | tf_op | source)
XLA Modules:
  0.0 755.2 jit_solution(8258046197964841338)
XLA Ops:
  6.5 2.7 fusion.61
  9.2 4.1 collective-permute-start
  13.3 1.9 collective-permute-start.1
  19.3 17.0 %collective-permute-done = f32[128,2048]{1,0:T(8,128)S(1)} collective-permute-done((f32[128,2048]{1,0:T(8,128)}, f32[128,2048]{1,0:T(8,128)S(1)}, u32[]{:S(2)}, u32[]{:S(2)}) %collective-permute-start) | collective-permute-done | bytes 1048608 | tf_op jit(solution)/shard_map/ppermute | solution.py:18
  36.2 1.8 collective-permute-done.1
  38.1 3.8 pad_maximum_fusion.4
  41.9 3.3 fusion.2
  45.2 5.3 copy.22
  54.2 4.0 collective-permute-done.3
  58.2 2.7 pad_maximum_fusion
  61.4 3.7 fusion.5
  65.1 5.4 copy.23
  70.5 4.6 gather_fusion
  75.1 1.7 select_select_fusion.1
  76.9 3.4 gather_fusion.2
  81.2 158.6 %all-reduce.16.cloned.1.call-done = f32[256,2048]{1,0:T(8,128)} async-done(((f32[256,2048]{1,0:T(8,128)}), f32[256,2048]{1,0:T(8,128)}) %all-reduce.16.cloned.1.call-update) | async-done | bytes 2097168 | tf_op jit(solution)/shard_map/psum | solution.py:83
  239.8 1.9 copy.14
  243.9 65.5 %all-reduce.22.cloned.1.call-done = (f32[256,512]{1,0:T(8,128)}, f32[256,256]{0,1:T(8,128)}) async-done(((f32[256,512]{1,0:T(8,128)}, f32[256,256]{0,1:T(8,128)}), (f32[256,512]{1,0:T(8,128)}, f32[256,256]{0,1:T(8,128)})) %all-reduce.22.cloned.1.call-update) | async-done | bytes 786448 | tf_op jit(solution)/shard_map/psum | solution.py:85
  311.7 11.7 %cholesky.130 = f32[128,128]{1,0:T(8,128)S(1)} custom-call(f32[128,128]{1,0:T(8,128)S(1)} %cholesky.194), custom_call_target="Cholesky" | custom-call | tf_op jit(solution)/shard_map/jit(cholesky)/cholesky | solution.py:87
  323.5 9.8 %custom-call.15 = f32[1,128,128]{1,2,0:T(8,128)S(1)} custom-call(f32[1,128,128]{2,1,0:T(8,128)S(1)} %get-tuple-element.79), custom_call_target="InvertDiagBlocksLowerTriangular" | custom-call | tf_op jit(solution)/shard_map/jit(cholesky)/cholesky | solution.py:87
  333.8 11.7 %cholesky.147 = f32[128,128]{1,0:T(8,128)S(1)} custom-call(f32[128,128]{1,0:T(8,128)S(1)} %convolution_subtract_fusion.7), custom_call_target="Cholesky" | custom-call | tf_op jit(solution)/shard_map/jit(cholesky)/cholesky | solution.py:87
  348.2 4.1 while.4
  349.1 1.3 bitcast_dynamic-update-slice_fusion.4
  352.4 19.7 %custom-call.16 = f32[2,128,128]{1,2,0:T(8,128)S(1)} custom-call(f32[2,128,128]{2,1,0:T(8,128)S(1)} %get-tuple-element.24), custom_call_target="InvertDiagBlocksLowerTriangular" | custom-call | tf_op jit(solution)/shard_map/jit(_cho_solve)/triangular_solve | solution.py:88
  374.5 5.3 convolution_subtract_fusion.1
  380.0 2.4 collective-permute-start.4
  382.5 3.4 collective-permute-start.5
  385.9 18.9 %collective-permute-done.4 = f32[128,2048]{1,0:T(8,128)S(1)} collective-permute-done((f32[128,2048]{1,0:T(8,128)S(1)}, f32[128,2048]{1,0:T(8,128)S(1)}, u32[]{:S(2)}, u32[]{:S(2)}) %collective-permute-start.4) | collective-permute-done | bytes 1048608 | tf_op jit(solution)/shard_map/ppermute | solution.py:18
  404.8 2.3 collective-permute-done.5
  407.1 2.7 pad_maximum_fusion.2
  409.8 3.3 fusion.8
  413.0 5.3 copy.24
  422.1 2.1 collective-permute-done.7
  424.2 2.7 pad_maximum_fusion.1
  427.4 3.7 fusion.11
  431.1 5.4 copy.25
  436.5 4.6 gather_fusion.3
  441.1 1.7 select_select_fusion
  442.8 3.4 gather_fusion.5
  447.2 159.6 %all-reduce.18.cloned.1.call-done = f32[256,2048]{1,0:T(8,128)} async-done(((f32[256,2048]{1,0:T(8,128)}), f32[256,2048]{1,0:T(8,128)}) %all-reduce.18.cloned.1.call-update) | async-done | bytes 2097168 | tf_op jit(solution)/shard_map/psum | solution.py:83
  606.8 2.3 copy.19
  611.0 65.8 %all-reduce.20.cloned.1.call-done = (f32[256,512]{1,0:T(8,128)}, f32[256,256]{0,1:T(8,128)}) async-done(((f32[256,512]{1,0:T(8,128)}, f32[256,256]{0,1:T(8,128)}), (f32[256,512]{1,0:T(8,128)}, f32[256,256]{0,1:T(8,128)})) %all-reduce.20.cloned.1.call-update) | async-done | bytes 786448 | tf_op jit(solution)/shard_map/psum | solution.py:85
  679.1 11.7 %cholesky.164 = f32[128,128]{1,0:T(8,128)S(1)} custom-call(f32[128,128]{1,0:T(8,128)S(1)} %cholesky.197), custom_call_target="Cholesky" | custom-call | tf_op jit(solution)/shard_map/jit(cholesky)/cholesky | solution.py:87
  690.9 9.8 %custom-call.17 = f32[1,128,128]{1,2,0:T(8,128)S(1)} custom-call(f32[1,128,128]{2,1,0:T(8,128)S(1)} %get-tuple-element.75), custom_call_target="InvertDiagBlocksLowerTriangular" | custom-call | tf_op jit(solution)/shard_map/jit(cholesky)/cholesky | solution.py:87
  701.2 11.7 %cholesky.181 = f32[128,128]{1,0:T(8,128)S(1)} custom-call(f32[128,128]{1,0:T(8,128)S(1)} %convolution_subtract_fusion.6), custom_call_target="Cholesky" | custom-call | tf_op jit(solution)/shard_map/jit(cholesky)/cholesky | solution.py:87
  715.5 3.9 while.5
  719.5 19.8 %custom-call.18 = f32[2,128,128]{1,2,0:T(8,128)S(1)} custom-call(f32[2,128,128]{2,1,0:T(8,128)S(1)} %get-tuple-element.25), custom_call_target="InvertDiagBlocksLowerTriangular" | custom-call | tf_op jit(solution)/shard_map/jit(_cho_solve)/triangular_solve | solution.py:88
  741.8 6.7 convolution_subtract_fusion
  (110 shorter events, 38.0 us)
Async XLA Ops:
  6.5 8.7 %copy-start.5 = (s32[2,256]{1,0:T(2,128)S(1)}, s32[2,256]{1,0:T(2,128)}, u32[]{:S(2)}) copy-start(s32[2,256]{1,0:T(2,128)} %param.17) | copy-start | bytes 6148
  6.5 233.3 %all-reduce.16.cloned.1.call-start = ((), (), s32[]{:S(2)}) async-start(), calls=%async_computation | async-start | bytes 4194304 | tf_op jit(solution)/shard_map/psum | solution.py:83
  9.2 27.0 %collective-permute-start = (f32[128,2048]{1,0:T(8,128)}, f32[128,2048]{1,0:T(8,128)S(1)}, u32[]{:S(2)}, u32[]{:S(2)}) collective-permute-start(f32[128,2048]{1,0:T(8,128)} %get-tuple-element.67), channel_id=1, source_target_pairs={{8,0},{16,8},{24,16},{32,24},{40,32},{48,40},{56,48},{64,56},{72,6... | collective-permute-start | bytes 3145736 | tf_op jit(solution)/shard_map/ppermute | solution.py:18
  13.3 24.8 %collective-permute-start.1 = (f32[128,2048]{1,0:T(8,128)S(1)}, f32[128,2048]{1,0:T(8,128)}, u32[]{:S(2)}, u32[]{:S(2)}) collective-permute-start(f32[128,2048]{1,0:T(8,128)S(1)} %get-tuple-element.66), channel_id=1, source_target_pairs={{0,8},{8,16},{16,24},{24,32},{32,40},{40,48},{48,56},{56,64},{64,7... | collective-permute-start | bytes 3145736 | tf_op jit(solution)/shard_map/ppermute | solution.py:15
  19.3 22.6 %copy-start = (f32[512,2048]{1,0:T(8,128)S(1)}, f32[512,2048]{1,0:T(8,128)}, u32[]{:S(2)}) copy-start(f32[512,2048]{1,0:T(8,128)} %param.14) | copy-start | bytes 12582916
  51.6 2.6 collective-permute-start.2
  52.9 5.3 collective-permute-start.3
  76.8 232.6 %all-reduce.22.cloned.1.call-start = ((), (), s32[]{:S(2)}) async-start(), calls=%async_computation.3 | async-start | bytes 1572864 | tf_op jit(solution)/shard_map/psum | solution.py:85
  81.2 162.7 %copy-start.6 = (f32[2,256]{1,0:T(2,128)S(1)}, f32[2,256]{1,0:T(2,128)}, u32[]{:S(2)}) copy-start(f32[2,256]{1,0:T(2,128)} %param.18) | copy-start | bytes 6148
  243.6 363.2 %all-reduce.18.cloned.1.call-start = ((), (), s32[]{:S(2)}) async-start(), calls=%async_computation.1 | async-start | bytes 4194304 | tf_op jit(solution)/shard_map/psum | solution.py:83
  309.4 62.7 %copy-start.3 = (f32[256,512]{1,0:T(8,128)S(1)}, f32[256,512]{1,0:T(8,128)}, u32[]{:S(2)}) copy-start(f32[256,512]{1,0:T(8,128)} %get-tuple-element.48) | copy-start | bytes 1572868
  310.4 64.0 %copy-start.1 = (f32[256,2048]{1,0:T(8,128)S(1)}, f32[256,2048]{1,0:T(8,128)}, u32[]{:S(2)}) copy-start(f32[256,2048]{1,0:T(8,128)} %all-reduce.16.cloned.1.call-done) | copy-start | bytes 6291460
  380.0 24.8 %collective-permute-start.4 = (f32[128,2048]{1,0:T(8,128)S(1)}, f32[128,2048]{1,0:T(8,128)S(1)}, u32[]{:S(2)}, u32[]{:S(2)}) collective-permute-start(f32[128,2048]{1,0:T(8,128)S(1)} %get-tuple-element.61), channel_id=1, source_target_pairs={{8,0},{16,8},{24,16},{32,24},{40,32},{48,40},{56,48},{64,56},{72,6... | collective-permute-start | bytes 3145736 | tf_op jit(solution)/shard_map/ppermute | solution.py:18
  382.5 24.6 %collective-permute-start.5 = (f32[128,2048]{1,0:T(8,128)S(1)}, f32[128,2048]{1,0:T(8,128)}, u32[]{:S(2)}, u32[]{:S(2)}) collective-permute-start(f32[128,2048]{1,0:T(8,128)S(1)} %get-tuple-element.60), channel_id=1, source_target_pairs={{0,8},{8,16},{16,24},{24,32},{32,40},{40,48},{48,56},{56,64},{64,7... | collective-permute-start | bytes 3145736 | tf_op jit(solution)/shard_map/ppermute | solution.py:15
  419.5 2.6 collective-permute-start.6
  420.8 3.4 collective-permute-start.7
  442.8 234.0 %all-reduce.20.cloned.1.call-start = ((), (), s32[]{:S(2)}) async-start(), calls=%async_computation.2 | async-start | bytes 1572864 | tf_op jit(solution)/shard_map/psum | solution.py:85
  676.8 62.5 %copy-start.4 = (f32[256,512]{1,0:T(8,128)S(1)}, f32[256,512]{1,0:T(8,128)}, u32[]{:S(2)}) copy-start(f32[256,512]{1,0:T(8,128)} %get-tuple-element.46) | copy-start | bytes 1572868
  677.8 63.9 %copy-start.2 = (f32[256,2048]{1,0:T(8,128)S(1)}, f32[256,2048]{1,0:T(8,128)}, u32[]{:S(2)}) copy-start(f32[256,2048]{1,0:T(8,128)} %all-reduce.18.cloned.1.call-done) | copy-start | bytes 6291460
Sparse Core Ops, SparseCore 0:
  76.9 162.9 all-reduce.15
  243.7 65.6 all-reduce.21
  442.9 163.9 all-reduce.17
  611.1 65.6 all-reduce.19
where the time goes:
time: 763 us; the launch traced here: 755 us
  waiting for transfers between devices  496 us (65%)
  other arithmetic  148 us (19%)
  local copies, waits for them, and re-layouts  59.5 us (8%)
  matrix products  17.7 us (2%)
  starting transfers between devices  17.3 us (2%)
  between operations  16.5 us (2%)
    psum x2, waiting for transfers between devices, shards(): row_panel = lax.psum(row_part, 'row')  318 us
    psum x2, waiting for transfers between devices, shards(): col_panel, innov = lax.psum((col_part, block_part), 'col')  131 us
    another operation x14, other arithmetic, shards(): factor = jnp.linalg.cholesky(innov)  69.2 us
    ppermute x4, waiting for transfers between devices, extended(): lax.ppermute(lax.slice_in_dim(block, 0, width, axis=dim), axis, backward)  41.9 us
    another operation x5, other arithmetic, shards(): gain = jax.scipy.linalg.cho_solve((factor, True), col_panel.T).T  39.6 us
  transfers between devices with their start and end apart: 12, of which 10 were waited for; matrix products, arithmetic and copies ran while one was open for 2% of the time, Pallas kernels for 0%

commit v1 on v0

--- a/solution.py
+++ b/solution.py
@@ -80,7 +80,11 @@
         col_pick = jnp.clip(local_cols, 0, col_count - 1)
         row_part = jnp.where(owns_row[:, None], jnp.take(block, row_pick, axis=0), 0.0)
         col_part = jnp.where(owns_col[None, :], jnp.take(block, col_pick, axis=1), 0.0)
-        row_panel = lax.psum(row_part, "row")
+        row_panel = row_part
+        for hop in (1, 2, 4, 8, 16):
+            row_panel = row_panel + lax.ppermute(
+                row_panel, "row", [(dev, dev ^ hop) for dev in range(32)]
+            )
         block_part = jnp.where(owns_col[None, :], jnp.take(row_panel, col_pick, axis=1), 0.0)
         col_panel, innov = lax.psum((col_part, block_part), "col")
         innov = innov + jnp.diag(noise[cycle])

time: 763 us -> 1150 us (1.51)
  waiting for transfers between devices: 496 us -> 835 us
  starting transfers between devices: 17.3 us -> 55.9 us
    ppermute x0 -> x10, waiting for transfers between devices: none -> 617 us  [shards(): lax.ppermute(row_panel, 'row', [(dev, dev ^ hop) for dev in range(32)])]
    psum x2 -> x0, waiting for transfers between devices: 318 us -> none  [shards(): row_panel = lax.psum(row_part, 'row')]
    psum x2, waiting for transfers between devices: 131 us -> 172 us  [shards(): col_panel, innov = lax.psum((col_part, block_part), 'col')]
    ppermute x0 -> x10, starting transfers between devices: none -> 38.7 us  [shards(): lax.ppermute(row_panel, 'row', [(dev, dev ^ hop) for dev in range(32)])]
    ppermute x4, waiting for transfers between devices: 4.12 us -> 20.7 us  [extended(): lax.ppermute(lax.slice_in_dim(block, block.shape[dim] - width, None, axis...]
    ppermute x4, waiting for transfers between devices: 41.9 us -> 26.2 us  [extended(): lax.ppermute(lax.slice_in_dim(block, 0, width, axis=dim), axis, backward)]
  transfers between devices with their start and end apart: 12 -> 20, of which waited for: 10 -> 18; matrix products, arithmetic and copies ran while one was open for 2% -> 1% of each run, Pallas kernels for 0% -> 0%
where the time goes in v1:
time: 1150 us; the launch traced here: 1140 us
  waiting for transfers between devices  835 us (73%)
  other arithmetic  153 us (13%)
  local copies, waits for them, and re-layouts  62.6 us (5%)
  starting transfers between devices  55.9 us (5%)
  matrix products  17.7 us (2%)
  between operations  17.2 us (1%)
    ppermute x10, waiting for transfers between devices, shards(): lax.ppermute(row_panel, 'row', [(dev, dev ^ hop) for dev in range(32)])  617 us
    psum x2, waiting for transfers between devices, shards(): col_panel, innov = lax.psum((col_part, block_part), 'col')  172 us
    another operation x14, other arithmetic, shards(): factor = jnp.linalg.cholesky(innov)  69.3 us
    another operation x5, other arithmetic, shards(): gain = jax.scipy.linalg.cho_solve((factor, True), col_panel.T).T  39.7 us
    ppermute x10, starting transfers between devices, shards(): lax.ppermute(row_panel, 'row', [(dev, dev ^ hop) for dev in range(32)])  38.7 us
    ppermute x4, waiting for transfers between devices, extended(): lax.ppermute(lax.slice_in_dim(block, 0, width, axis=dim), axis, backward)  26.2 us
  transfers between devices with their start and end apart: 20, of which 18 were waited for; matrix products, arithmetic and copies ran while one was open for 1% of the time, Pallas kernels for 0%

profile of v1, /device:TPU:8, one launch (start us, length us, event | category | flops | bytes accessed | tf_op | source)
XLA Modules:
  0.0 1142.2 jit_solution(14769491890301104347)
XLA Ops:
  9.2 4.1 collective-permute-start
  19.3 17.0 %collective-permute-done = f32[128,2048]{1,0:T(8,128)S(1)} collective-permute-done((f32[128,2048]{1,0:T(8,128)}, f32[128,2048]{1,0:T(8,128)S(1)}, u32[]{:S(2)}, u32[]{:S(2)}) %collective-permute-start) | collective-permute-done | bytes 1048608 | tf_op jit(solution)/shard_map/ppermute | solution.py:18
  38.1 3.8 pad_maximum_fusion.4
  41.9 3.3 fusion.2
  45.2 5.4 copy.22
  54.2 4.0 collective-permute-done.3
  61.4 3.7 fusion.5
  65.1 5.4 copy.23
  70.4 4.6 gather_fusion
  75.4 44.7 %collective-permute-done.4 = f32[256,2048]{1,0:T(8,128)S(1)} collective-permute-done((f32[256,2048]{1,0:T(8,128)S(1)}, f32[256,2048]{1,0:T(8,128)S(1)}, u32[]{:S(2)}, u32[]{:S(2)}) %collective-permute-start.4) | collective-permute-done | bytes 2097184 | tf_op jit(solution)/shard_map/ppermute | solution.py:85
  120.5 3.5 collective-permute-start.5
  124.0 41.5 %collective-permute-done.5 = f32[256,2048]{1,0:T(8,128)S(1)} collective-permute-done((f32[256,2048]{1,0:T(8,128)S(1)}, f32[256,2048]{1,0:T(8,128)S(1)}, u32[]{:S(2)}, u32[]{:S(2)}) %collective-permute-start.5) | collective-permute-done | bytes 2097184 | tf_op jit(solution)/shard_map/ppermute | solution.py:85
  165.8 5.7 collective-permute-start.6
  171.5 43.6 %collective-permute-done.6 = f32[256,2048]{1,0:T(8,128)S(1)} collective-permute-done((f32[256,2048]{1,0:T(8,128)S(1)}, f32[256,2048]{1,0:T(8,128)S(1)}, u32[]{:S(2)}, u32[]{:S(2)}) %collective-permute-start.6) | collective-permute-done | bytes 2097184 | tf_op jit(solution)/shard_map/ppermute | solution.py:85
  215.5 5.1 collective-permute-start.7
  220.5 90.2 %collective-permute-done.7 = f32[256,2048]{1,0:T(8,128)S(1)} collective-permute-done((f32[256,2048]{1,0:T(8,128)S(1)}, f32[256,2048]{1,0:T(8,128)S(1)}, u32[]{:S(2)}, u32[]{:S(2)}) %collective-permute-start.7) | collective-permute-done | bytes 2097184 | tf_op jit(solution)/shard_map/ppermute | solution.py:85
  311.0 5.7 collective-permute-start.8
  316.7 3.4 gather_fusion.2
  321.1 88.1 %collective-permute-done.8 = f32[256,2048]{1,0:T(8,128)} collective-permute-done((f32[256,2048]{1,0:T(8,128)S(1)}, f32[256,2048]{1,0:T(8,128)}, u32[]{:S(2)}, u32[]{:S(2)}) %collective-permute-start.8) | collective-permute-done | bytes 2097184 | tf_op jit(solution)/shard_map/ppermute | solution.py:85
  417.0 95.8 %all-reduce.16.cloned.1.call-done = (f32[256,512]{1,0:T(8,128)}, f32[256,256]{0,1:T(8,128)}) async-done(((f32[256,512]{1,0:T(8,128)}, f32[256,256]{0,1:T(8,128)}), (f32[256,512]{1,0:T(8,128)}, f32[256,256]{0,1:T(8,128)})) %all-reduce.16.cloned.1.call-update) | async-done | bytes 786448 | tf_op jit(solution)/shard_map/psum | solution.py:89
  515.0 11.7 %cholesky.130 = f32[128,128]{1,0:T(8,128)S(1)} custom-call(f32[128,128]{1,0:T(8,128)S(1)} %cholesky.194), custom_call_target="Cholesky" | custom-call | tf_op jit(solution)/shard_map/jit(cholesky)/cholesky | solution.py:91
  526.8 9.8 custom-call.15
  537.1 11.7 %cholesky.147 = f32[128,128]{1,0:T(8,128)S(1)} custom-call(f32[128,128]{1,0:T(8,128)S(1)} %convolution_subtract_fusion.7), custom_call_target="Cholesky" | custom-call | tf_op jit(solution)/shard_map/jit(cholesky)/cholesky | solution.py:91
  551.6 4.5 while.4
  556.2 19.7 %custom-call.16 = f32[2,128,128]{1,2,0:T(8,128)S(1)} custom-call(f32[2,128,128]{2,1,0:T(8,128)S(1)} %get-tuple-element.24), custom_call_target="InvertDiagBlocksLowerTriangular" | custom-call | tf_op jit(solution)/shard_map/jit(_cho_solve)/triangular_solve | solution.py:92
  578.3 5.3 convolution_subtract_fusion.1
  583.8 3.4 collective-permute-start.10
  589.8 18.9 %collective-permute-done.10 = f32[128,2048]{1,0:T(8,128)S(1)} collective-permute-done((f32[128,2048]{1,0:T(8,128)S(1)}, f32[128,2048]{1,0:T(8,128)S(1)}, u32[]{:S(2)}, u32[]{:S(2)}) %collective-permute-start.10) | collective-permute-done | bytes 1048608 | tf_op jit(solution)/shard_map/ppermute | solution.py:15
  617.6 5.4 copy.24
  632.0 3.9 fusion.11
  635.9 5.4 copy.25
  641.2 4.6 gather_fusion.3
  646.8 44.7 %collective-permute-done.13 = f32[256,2048]{1,0:T(8,128)S(1)} collective-permute-done((f32[256,2048]{1,0:T(8,128)S(1)}, f32[256,2048]{1,0:T(8,128)S(1)}, u32[]{:S(2)}, u32[]{:S(2)}) %collective-permute-start.13) | collective-permute-done | bytes 2097184 | tf_op jit(solution)/shard_map/ppermute | solution.py:85
  691.9 4.3 collective-permute-start.14
  696.2 42.7 %collective-permute-done.14 = f32[256,2048]{1,0:T(8,128)S(1)} collective-permute-done((f32[256,2048]{1,0:T(8,128)S(1)}, f32[256,2048]{1,0:T(8,128)S(1)}, u32[]{:S(2)}, u32[]{:S(2)}) %collective-permute-start.14) | collective-permute-done | bytes 2097184 | tf_op jit(solution)/shard_map/ppermute | solution.py:85
  740.9 44.3 %collective-permute-done.15 = f32[256,2048]{1,0:T(8,128)S(1)} collective-permute-done((f32[256,2048]{1,0:T(8,128)S(1)}, f32[256,2048]{1,0:T(8,128)S(1)}, u32[]{:S(2)}, u32[]{:S(2)}) %collective-permute-start.15) | collective-permute-done | bytes 2097184 | tf_op jit(solution)/shard_map/ppermute | solution.py:85
  785.6 4.3 collective-permute-start.16
  789.8 89.6 %collective-permute-done.16 = f32[256,2048]{1,0:T(8,128)S(1)} collective-permute-done((f32[256,2048]{1,0:T(8,128)S(1)}, f32[256,2048]{1,0:T(8,128)S(1)}, u32[]{:S(2)}, u32[]{:S(2)}) %collective-permute-start.16) | collective-permute-done | bytes 2097184 | tf_op jit(solution)/shard_map/ppermute | solution.py:85
  879.7 7.8 collective-permute-start.17
  887.5 3.4 gather_fusion.5
  891.9 87.2 %collective-permute-done.17 = f32[256,2048]{1,0:T(8,128)} collective-permute-done((f32[256,2048]{1,0:T(8,128)S(1)}, f32[256,2048]{1,0:T(8,128)}, u32[]{:S(2)}, u32[]{:S(2)}) %collective-permute-start.17) | collective-permute-done | bytes 2097184 | tf_op jit(solution)/shard_map/ppermute | solution.py:85
  987.0 76.1 %all-reduce.14.cloned.1.call-done = (f32[256,512]{1,0:T(8,128)}, f32[256,256]{0,1:T(8,128)}) async-done(((f32[256,512]{1,0:T(8,128)}, f32[256,256]{0,1:T(8,128)}), (f32[256,512]{1,0:T(8,128)}, f32[256,256]{0,1:T(8,128)})) %all-reduce.14.cloned.1.call-update) | async-done | bytes 786448 | tf_op jit(solution)/shard_map/psum | solution.py:89
  1065.2 11.7 %cholesky.164 = f32[128,128]{1,0:T(8,128)S(1)} custom-call(f32[128,128]{1,0:T(8,128)S(1)} %cholesky.197), custom_call_target="Cholesky" | custom-call | tf_op jit(solution)/shard_map/jit(cholesky)/cholesky | solution.py:91
  1077.0 9.8 custom-call.17
  1087.3 11.7 %cholesky.181 = f32[128,128]{1,0:T(8,128)S(1)} custom-call(f32[128,128]{1,0:T(8,128)S(1)} %convolution_subtract_fusion.6), custom_call_target="Cholesky" | custom-call | tf_op jit(solution)/shard_map/jit(cholesky)/cholesky | solution.py:91
  1101.8 4.1 while.5
  1105.9 19.9 %custom-call.18 = f32[2,128,128]{1,2,0:T(8,128)S(1)} custom-call(f32[2,128,128]{2,1,0:T(8,128)S(1)} %get-tuple-element.25), custom_call_target="InvertDiagBlocksLowerTriangular" | custom-call | tf_op jit(solution)/shard_map/jit(_cho_solve)/triangular_solve | solution.py:92
  1128.3 6.7 convolution_subtract_fusion
  (133 shorter events, 82.5 us)
Async XLA Ops:
  6.5 8.7 copy-start.5
  6.5 506.3 %all-reduce.16.cloned.1.call-start = ((), (), s32[]{:S(2)}) async-start(), calls=%async_computation.1 | async-start | bytes 1572864 | tf_op jit(solution)/shard_map/psum | solution.py:89
  9.2 27.0 %collective-permute-start = (f32[128,2048]{1,0:T(8,128)}, f32[128,2048]{1,0:T(8,128)S(1)}, u32[]{:S(2)}, u32[]{:S(2)}) collective-permute-start(f32[128,2048]{1,0:T(8,128)} %get-tuple-element.67), channel_id=1, source_target_pairs={{8,0},{16,8},{24,16},{32,24},{40,32},{48,40},{56,48},{64,56},{72,6... | collective-permute-start | bytes 3145736 | tf_op jit(solution)/shard_map/ppermute | solution.py:18
  13.3 24.8 %collective-permute-start.1 = (f32[128,2048]{1,0:T(8,128)S(1)}, f32[128,2048]{1,0:T(8,128)}, u32[]{:S(2)}, u32[]{:S(2)}) collective-permute-start(f32[128,2048]{1,0:T(8,128)S(1)} %get-tuple-element.66), channel_id=1, source_target_pairs={{0,8},{8,16},{16,24},{24,32},{32,40},{40,48},{48,56},{56,64},{64,7... | collective-permute-start | bytes 3145736 | tf_op jit(solution)/shard_map/ppermute | solution.py:15
  19.3 22.6 %copy-start = (f32[512,2048]{1,0:T(8,128)S(1)}, f32[512,2048]{1,0:T(8,128)}, u32[]{:S(2)}) copy-start(f32[512,2048]{1,0:T(8,128)} %param.14) | copy-start | bytes 12582916
  51.6 2.6 collective-permute-start.2
  52.9 5.3 collective-permute-start.3
  75.3 44.8 %collective-permute-start.4 = (f32[256,2048]{1,0:T(8,128)S(1)}, f32[256,2048]{1,0:T(8,128)S(1)}, u32[]{:S(2)}, u32[]{:S(2)}) collective-permute-start(f32[256,2048]{1,0:T(8,128)S(1)} %select_select_fusion.1), channel_id=1, source_target_pairs={{0,8},{8,0},{16,24},{24,16},{32,40},{40,32},{48,56},{56,48},{64,72... | collective-permute-start | bytes 6291464 | tf_op jit(solution)/shard_map/ppermute | solution.py:85
  120.5 45.0 %collective-permute-start.5 = (f32[256,2048]{1,0:T(8,128)S(1)}, f32[256,2048]{1,0:T(8,128)S(1)}, u32[]{:S(2)}, u32[]{:S(2)}) collective-permute-start(f32[256,2048]{1,0:T(8,128)S(1)} %fusion.80), channel_id=1, source_target_pairs={{0,16},{8,24},{16,0},{24,8},{32,48},{40,56},{48,32},{56,40},{64,80... | collective-permute-start | bytes 6291464 | tf_op jit(solution)/shard_map/ppermute | solution.py:85
  165.8 49.3 %collective-permute-start.6 = (f32[256,2048]{1,0:T(8,128)S(1)}, f32[256,2048]{1,0:T(8,128)S(1)}, u32[]{:S(2)}, u32[]{:S(2)}) collective-permute-start(f32[256,2048]{1,0:T(8,128)S(1)} %add.177), channel_id=1, source_target_pairs={{0,32},{8,40},{16,48},{24,56},{32,0},{40,8},{48,16},{56,24},{64,96... | collective-permute-start | bytes 6291464 | tf_op jit(solution)/shard_map/ppermute | solution.py:85
  215.5 95.3 %collective-permute-start.7 = (f32[256,2048]{1,0:T(8,128)S(1)}, f32[256,2048]{1,0:T(8,128)S(1)}, u32[]{:S(2)}, u32[]{:S(2)}) collective-permute-start(f32[256,2048]{1,0:T(8,128)S(1)} %add.178), channel_id=1, source_target_pairs={{0,64},{8,72},{16,80},{24,88},{32,96},{40,104},{48,112},{56,120},{... | collective-permute-start | bytes 6291464 | tf_op jit(solution)/shard_map/ppermute | solution.py:85
  311.0 10.1 copy-start.2
  311.0 98.2 %collective-permute-start.8 = (f32[256,2048]{1,0:T(8,128)S(1)}, f32[256,2048]{1,0:T(8,128)}, u32[]{:S(2)}, u32[]{:S(2)}) collective-permute-start(f32[256,2048]{1,0:T(8,128)S(1)} %add.179), channel_id=1, source_target_pairs={{0,128},{8,136},{16,144},{24,152},{32,160},{40,168},{48,176},{56,1... | collective-permute-start | bytes 6291464 | tf_op jit(solution)/shard_map/ppermute | solution.py:85
  411.7 5.3 copy-start.6
  417.0 646.1 %all-reduce.14.cloned.1.call-start = ((), (), s32[]{:S(2)}) async-start(), calls=%async_computation | async-start | bytes 1572864 | tf_op jit(solution)/shard_map/psum | solution.py:89
  512.8 63.0 %copy-start.3 = (f32[256,512]{1,0:T(8,128)S(1)}, f32[256,512]{1,0:T(8,128)}, u32[]{:S(2)}) copy-start(f32[256,512]{1,0:T(8,128)} %get-tuple-element.48) | copy-start | bytes 1572868
  583.8 24.8 %collective-permute-start.10 = (f32[128,2048]{1,0:T(8,128)S(1)}, f32[128,2048]{1,0:T(8,128)S(1)}, u32[]{:S(2)}, u32[]{:S(2)}) collective-permute-start(f32[128,2048]{1,0:T(8,128)S(1)} %get-tuple-element.60), channel_id=1, source_target_pairs={{0,8},{8,16},{16,24},{24,32},{32,40},{40,48},{48,56},{56,64},{64,7... | collective-permute-start | bytes 3145736 | tf_op jit(solution)/shard_map/ppermute | solution.py:15
  587.2 24.6 %collective-permute-start.9 = (f32[128,2048]{1,0:T(8,128)S(1)}, f32[128,2048]{1,0:T(8,128)}, u32[]{:S(2)}, u32[]{:S(2)}) collective-permute-start(f32[128,2048]{1,0:T(8,128)S(1)} %get-tuple-element.61), channel_id=1, source_target_pairs={{8,0},{16,8},{24,16},{32,24},{40,32},{48,40},{56,48},{64,56},{72,6... | collective-permute-start | bytes 3145736 | tf_op jit(solution)/shard_map/ppermute | solution.py:18
  624.1 2.6 collective-permute-start.11
  625.4 3.4 collective-permute-start.12
  646.1 45.4 %collective-permute-start.13 = (f32[256,2048]{1,0:T(8,128)S(1)}, f32[256,2048]{1,0:T(8,128)S(1)}, u32[]{:S(2)}, u32[]{:S(2)}) collective-permute-start(f32[256,2048]{1,0:T(8,128)S(1)} %select_select_fusion), channel_id=1, source_target_pairs={{0,8},{8,0},{16,24},{24,16},{32,40},{40,32},{48,56},{56,48},{64,72... | collective-permute-start | bytes 6291464 | tf_op jit(solution)/shard_map/ppermute | solution.py:85
  691.9 47.0 %collective-permute-start.14 = (f32[256,2048]{1,0:T(8,128)S(1)}, f32[256,2048]{1,0:T(8,128)S(1)}, u32[]{:S(2)}, u32[]{:S(2)}) collective-permute-start(f32[256,2048]{1,0:T(8,128)S(1)} %fusion.79), channel_id=1, source_target_pairs={{0,16},{8,24},{16,0},{24,8},{32,48},{40,56},{48,32},{56,40},{64,80... | collective-permute-start | bytes 6291464 | tf_op jit(solution)/shard_map/ppermute | solution.py:85
  739.3 46.0 %collective-permute-start.15 = (f32[256,2048]{1,0:T(8,128)S(1)}, f32[256,2048]{1,0:T(8,128)S(1)}, u32[]{:S(2)}, u32[]{:S(2)}) collective-permute-start(f32[256,2048]{1,0:T(8,128)S(1)} %add.187), channel_id=1, source_target_pairs={{0,32},{8,40},{16,48},{24,56},{32,0},{40,8},{48,16},{56,24},{64,96... | collective-permute-start | bytes 6291464 | tf_op jit(solution)/shard_map/ppermute | solution.py:85
  785.6 93.8 %collective-permute-start.16 = (f32[256,2048]{1,0:T(8,128)S(1)}, f32[256,2048]{1,0:T(8,128)S(1)}, u32[]{:S(2)}, u32[]{:S(2)}) collective-permute-start(f32[256,2048]{1,0:T(8,128)S(1)} %add.188), channel_id=1, source_target_pairs={{0,64},{8,72},{16,80},{24,88},{32,96},{40,104},{48,112},{56,120},{... | collective-permute-start | bytes 6291464 | tf_op jit(solution)/shard_map/ppermute | solution.py:85
  879.7 12.2 %copy-start.1 = (f32[256,2048]{1,0:T(8,128)}, f32[256,2048]{1,0:T(8,128)S(1)}, u32[]{:S(2)}) copy-start(f32[256,2048]{1,0:T(8,128)S(1)} %add.189) | copy-start | bytes 6291460
  879.7 99.3 %collective-permute-start.17 = (f32[256,2048]{1,0:T(8,128)S(1)}, f32[256,2048]{1,0:T(8,128)}, u32[]{:S(2)}, u32[]{:S(2)}) collective-permute-start(f32[256,2048]{1,0:T(8,128)S(1)} %add.189), channel_id=1, source_target_pairs={{0,128},{8,136},{16,144},{24,152},{32,160},{40,168},{48,176},{56,1... | collective-permute-start | bytes 6291464 | tf_op jit(solution)/shard_map/ppermute | solution.py:85
  1063.0 62.8 %copy-start.4 = (f32[256,512]{1,0:T(8,128)S(1)}, f32[256,512]{1,0:T(8,128)}, u32[]{:S(2)}) copy-start(f32[256,512]{1,0:T(8,128)} %get-tuple-element.46) | copy-start | bytes 1572868
Sparse Core Ops, SparseCore 0:
  417.1 95.7 all-reduce.15
  987.1 75.8 all-reduce.13
